TPU v7x, 32 devices: a whole 2x2x4 slice. The times are simulated.
32 devices in a mesh: seg: 8 (over z, x), head: 4 (over y, core).
Axes of the slice: x: 2, y: 2, z: 4, core: 2. Of those that a mesh axis runs over, the one named last changes fastest.
Arguments:
- q_heads: bfloat16 [6144, 2048], P('seg', 'head'), may hold values from -6 to 6
- k_heads: bfloat16 [6144, 2048], P('seg', 'head'), may hold values from -6 to 6
- v_heads: bfloat16 [6144, 2048], P('seg', 'head'), may hold values from -600 to 600
- log_decay: float32 [16, 6144], P('head', 'seg'), may hold values from -1 to 0
- parent: int32 [8], replicated, may hold values from -1 to 7, as said below
- norm_gain: float32 [2048], P('head'), may hold values from 0.1 to 1.9
- w_out: bfloat16 [2048, 6144], P('head'), may hold values from -0.125 to 0.125
Outputs:
- mixed: bfloat16 [6144, 6144], P(('seg', 'head'))
Inputs may be any that keep to these rules, and one draw needn't show every extreme that they name: A segment's parent is a root or a segment whose parent is a root; the tree has three levels, and the third is never empty.
All inputs are finite; a program needn't handle non-finite values.
Results may differ from a plain program's by a relative error of at most 0.0051.
Values sent between devices are 32-bit elements; how exact they have to be, the bound alone decides.
A program may use at most 128 MiB of HBM per device.

v0:
```python
import jax
import jax.numpy as jnp
from jax import lax
from jax.sharding import PartitionSpec as P


def per_device(q_heads, k_heads, v_heads, log_decay, parent, norm_gain, w_out):
    segment_len = q_heads.shape[0]
    head_count = log_decay.shape[0]
    head_width = q_heads.shape[1] // head_count
    queries = q_heads.reshape(segment_len, head_count, head_width)
    key_rows = k_heads.reshape(segment_len, head_count, head_width)
    values = v_heads.reshape(segment_len, head_count, head_width)
    running = jnp.cumsum(log_decay, axis=1)
    segment_total = running[:, -1]
    key_weight = jnp.exp(segment_total[:, None] - running)
    weighted = key_rows.astype(jnp.float32) * key_weight.T[:, :, None]
    local_state = jnp.einsum(
        "shd,she->hde", weighted, values.astype(jnp.float32), precision=lax.Precision.HIGHEST
    )
    scores = jnp.einsum("thd,shd->hts", queries, key_rows, preferred_element_type=jnp.float32)
    row_index = lax.broadcasted_iota(jnp.int32, (segment_len, segment_len), 0)
    col_index = lax.broadcasted_iota(jnp.int32, (segment_len, segment_len), 1)
    causal = row_index >= col_index
    log_gap = running[:, :, None] - running[:, None, :]
    decay_factor = jnp.where(causal[None], jnp.exp(jnp.minimum(log_gap, 0.0)), 0.0)
    weights = (scores * head_width ** (-0.5) * decay_factor).astype(jnp.bfloat16)
    within = jnp.einsum("hts,she->the", weights, values, preferred_element_type=jnp.float32)
    own_index = lax.axis_index("seg")
    parent_id = parent[own_index]
    grand_id = jnp.where(parent_id >= 0, parent[jnp.maximum(parent_id, 0)], -1)
    states = lax.all_gather(local_state[None], "seg", axis=0, tiled=True)
    totals = lax.all_gather(segment_total[None], "seg", axis=0, tiled=True)
    segment_ids = jnp.arange(states.shape[0], dtype=jnp.int32)
    is_parent = segment_ids == parent_id
    is_grand = segment_ids == grand_id
    parent_sum = jnp.sum(jnp.where(is_parent[:, None, None, None], states, 0.0), axis=0)
    grand_sum = jnp.sum(jnp.where(is_grand[:, None, None, None], states, 0.0), axis=0)
    parent_total = jnp.sum(jnp.where(is_parent[:, None], totals, 0.0), axis=0)
    parent_sum, grand_sum, parent_total = (parent_sum, grand_sum, parent_total)
    prefix = jnp.exp(parent_total)[:, None, None] * grand_sum + parent_sum
    prefix_term = (
        jnp.einsum(
            "thd,hde->the", queries.astype(jnp.float32), prefix, precision=lax.Precision.HIGHEST
        )
        * jnp.exp(running).T[:, :, None]
    )
    attention = (prefix_term + within).reshape(segment_len, head_count * head_width)
    squares = lax.psum(jnp.sum(attention * attention, axis=1), "head")
    total_features = head_count * head_width * lax.axis_size("head")
    inverse = 1.0 / jnp.sqrt(squares / total_features + 1e-06)
    normed = (attention * inverse[:, None] * norm_gain[None, :]).astype(jnp.bfloat16)
    mixed = lax.psum_scatter(
        jnp.dot(normed, w_out, preferred_element_type=jnp.float32),
        "head",
        scatter_dimension=0,
        tiled=True,
    )
    return mixed.astype(jnp.bfloat16)


def solution(mesh):
    return jax.shard_map(
        per_device,
        mesh=mesh,
        in_specs=(
            P("seg", "head"),
            P("seg", "head"),
            P("seg", "head"),
            P("head", "seg"),
            P(),
            P("head"),
            P("head", None),
        ),
        out_specs=P(("seg", "head"), None),
        check_vma=False,
    )
```

profile of v0, /device:TPU:0, one launch (start us, length us, event | category | flops | bytes accessed | tf_op | source)
XLA Modules:
  0.0 234.6 jit_solution(15167253058687618074)
XLA Ops:
  6.5 0.8 reshape.72
  7.3 1.1 reduce-window.6
  8.5 0.2 slice_reduce_fusion
  8.6 0.2 reduce-window.9
  8.9 0.2 slice_reduce_fusion.1
  9.2 1.4 copy.31
  10.6 1.4 copy.32
  12.0 1.7 fusion.6
  13.8 0.6 dynamic_slice.6
  15.7 0.6 dynamic_slice.7
  16.2 0.6 dynamic-slice
  17.5 0.2 dynamic-update-slice
  17.7 23.5 %all-reduce = f32[32]{0:T(128)S(1)} all-reduce(f32[32]{0:T(128)S(1)} %dynamic-update-slice), channel_id=2, replica_groups=mesh['seg'=8,'head'=4] {'seg'}, use_global_device_ids=true, to_apply=%add | all-reduce | flops 32 | bytes 256
  41.3 0.7 iota_compare_fusion.2
  42.6 0.2 iota_compare_fusion
  42.8 5.6 %fusion = f32[4,768,128]{1,2,0:T(8,128)} fusion(bf16[768,4,128]{0,2,1:T(8,128)(2,1)S(1)} %bitcast.52, f32[4,768]{1,0:T(4,128)S(1)} %get-tuple-element.8, pred[768,768]{1,0:T(8,128)(4,1)S(1)} %iota_compare_fusion, bf16[768,4,128]{0,2,1:T(8,128)(2,1)S(1)} %bitcast.50, bf16[768,512]{1,0:T(8,128)(2,1)S(1)} %copy-done), kind=kOutput, calls=%fused_computation.1 | convolution fusion | flops 1222115328 | bytes 4534272 | tf_op jit(solution)/shard_map/hts,she->the/dot_general | solution.py:28
  48.3 17.5 %all-gather.4.cloned.1.call-done = f32[32,128,128]{2,1,0:T(8,128)} async-done(((f32[4,128,128]{2,1,0:T(8,128)}), f32[32,128,128]{2,1,0:T(8,128)}) %all-gather.4.cloned.1.call-update) | async-done | bytes 2097168 | tf_op jit(solution)/shard_map/all_gather | solution.py:32
  65.9 2.1 select_reduce_fusion.1
  68.0 1.1 multiply_reduce_fusion
  69.1 5.7 %psum.7 = f32[768]{0:T(1024)S(1)} all-reduce(f32[768]{0:T(1024)S(1)} %get-tuple-element.9), channel_id=1, replica_groups=mesh['seg'=8,'head'=4] {'head'}, use_global_device_ids=true, to_apply=%region_6.7 | all-reduce | flops 768 | bytes 6144 | tf_op jit(solution)/shard_map/psum | solution.py:49
  74.8 0.2 fusion.5
  75.0 11.9 %fusion.21 = f32[768,6144]{1,0:T(8,128)} fusion(bf16[768,512]{0,1:T(8,128)(2,1)S(1)} %fusion.5, bf16[512,6144]{1,0:T(8,128)(2,1)} %param.13), kind=kOutput, calls=%fused_computation.36 | convolution fusion | flops 4831838208 | bytes 25952256 | tf_op jit(solution)/shard_map/dot_general | solution.py:54
  87.0 136.8 %reduce-scatter.2.cloned.1.call-done = f32[192,6144]{1,0:T(8,128)} async-done(((f32[768,6144]{1,0:T(8,128)}), f32[192,6144]{1,0:T(8,128)}) %reduce-scatter.2.cloned.1.call-update) | async-done | bytes 4718608 | tf_op jit(solution)/shard_map/reduce_scatter | solution.py:53
  223.7 4.1 %convert_element_type.17 = bf16[192,6144]{1,0:T(8,128)(2,1)} convert(f32[192,6144]{1,0:T(8,128)} %reduce-scatter.2.cloned.1.call-done) | non-fusion elementwise | flops 1179648 | bytes 7077888 | tf_op jit(solution)/shard_map/convert_element_type | solution.py:59
  (23 shorter events, 0.5 us)
Async XLA Ops:
  6.5 36.2 %copy-start = (bf16[768,512]{1,0:T(8,128)(2,1)S(1)}, bf16[768,512]{1,0:T(8,128)(2,1)}, u32[]{:S(2)}) copy-start(bf16[768,512]{1,0:T(8,128)(2,1)} %param.7) | copy-start | bytes 2359300
  6.5 59.3 %all-gather.4.cloned.1.call-start = ((), (), s32[]{:S(2)}) async-start(), calls=%async_computation.2 | async-start | bytes 2359296 | tf_op jit(solution)/shard_map/all_gather | solution.py:32
  9.2 4.6 %copy-start.3 = (s32[8]{0:T(128)S(1)}, s32[8]{0:T(128)}, u32[]{:S(2)}) copy-start(s32[8]{0:T(128)} %param.11) | copy-start | bytes 100
  9.2 7.1 %copy-start.4 = (u32[32]{0:T(128)S(1)}, u32[32]{0:T(128)}, u32[]{:S(2)}) copy-start(u32[32]{0:T(128)} %constant.29) | copy-start | bytes 388
  13.7 210.0 %reduce-scatter.2.cloned.1.call-start = ((), (), s32[]{:S(2)}) async-start(), calls=%async_computation.1 | async-start | bytes 23592960 | tf_op jit(solution)/shard_map/reduce_scatter | solution.py:53
  65.9 2.1 copy-start.1
  68.0 6.8 %copy-start.2 = (f32[512]{0:T(512)S(1)}, f32[512]{0:T(512)}, u32[]{:S(2)}) copy-start(f32[512]{0:T(512)} %param.12) | copy-start | bytes 6148
Sparse Core Ops, SparseCore 0:
  13.8 51.9 all-gather.3
  87.1 136.6 reduce-scatter.1
where the time goes:
time: 235 us
  waiting for transfers between devices  154 us (66%)
  blocking collectives  29.1 us (12%)
  matrix products  20.2 us (9%)
  between operations  16 us (7%)
  other arithmetic  8.75 us (4%)
  local copies, waits for them, and re-layouts  6.08 us (3%)
    reduce_scatter x1, waiting for transfers between devices, per_device(): lax.psum_scatter(jnp.dot(normed, w_out, preferred_element_type=jnp.float3...  137 us
    unnamed x1, blocking collectives  23.5 us
    all_gather x1, waiting for transfers between devices, per_device(): states = lax.all_gather(local_state[None], 'seg', axis=0, tiled=True)  17.5 us
    dot_general x1, matrix products, per_device(): jnp.dot(normed, w_out, preferred_element_type=jnp.float32)  11.9 us
    psum x1, blocking collectives, per_device(): squares = lax.psum(jnp.sum(attention * attention, axis=1), 'head')  5.67 us
    dot_general x1, matrix products, per_device(): jnp.einsum('hts,she->the', weights, values, preferred_element_type=jnp.fl...  5.55 us
  transfers between devices with their start and end apart: 2, of which 2 were waited for; matrix products, arithmetic and copies ran while one was open for 4% of the time, Pallas kernels for 0%

commit v1 on v0

--- a/solution.py
+++ b/solution.py
@@ -2,6 +2,22 @@
 import jax.numpy as jnp
 from jax import lax
 from jax.sharding import PartitionSpec as P
+
+
+def gather_around(x, axis, dim):
+    ways, here, lap = (lax.axis_size(axis), lax.axis_index(axis), x.shape[dim])
+    shape = [n * ways if d == dim else n for d, n in enumerate(x.shape)]
+    full = lax.dynamic_update_slice_in_dim(jnp.zeros(shape, x.dtype), x, here * lap, axis=dim)
+    going_up = going_down = x
+    for far in range(1, ways // 2 + 1):
+        going_up = lax.ppermute(going_up, axis, [(d, (d + 1) % ways) for d in range(ways)])
+        full = lax.dynamic_update_slice_in_dim(full, going_up, (here - far) % ways * lap, axis=dim)
+        if 2 * far < ways:
+            going_down = lax.ppermute(going_down, axis, [(d, (d - 1) % ways) for d in range(ways)])
+            full = lax.dynamic_update_slice_in_dim(
+                full, going_down, (here + far) % ways * lap, axis=dim
+            )
+    return full
 
 
 def per_device(q_heads, k_heads, v_heads, log_decay, parent, norm_gain, w_out):
@@ -29,7 +45,7 @@
     own_index = lax.axis_index("seg")
     parent_id = parent[own_index]
     grand_id = jnp.where(parent_id >= 0, parent[jnp.maximum(parent_id, 0)], -1)
-    states = lax.all_gather(local_state[None], "seg", axis=0, tiled=True)
+    states = gather_around(local_state[None], "seg", 0)
     totals = lax.all_gather(segment_total[None], "seg", axis=0, tiled=True)
     segment_ids = jnp.arange(states.shape[0], dtype=jnp.int32)
     is_parent = segment_ids == parent_id

time: 235 us -> 248 us (1.055)
  starting transfers between devices: 0.04 us -> 13 us
  local copies, waits for them, and re-layouts: 6.08 us -> 10.3 us
  blocking collectives: 29.1 us -> 25.9 us
    all_gather x1 -> x0, waiting for transfers between devices: 17.5 us -> none  [per_device(): states = lax.all_gather(local_state[None], 'seg', axis=0, tiled=True)]
    ppermute x0 -> x7, waiting for transfers between devices: none -> 16 us  [the longest x3 12.3 us: gather_around(): lax.ppermute(going_down, axis, [(d, (d - 1) % ways) for d in range(ways)])]
    ppermute x0 -> x7, starting transfers between devices: none -> 13 us  [the longest x4 9.86 us: gather_around(): lax.ppermute(going_up, axis, [(d, (d + 1) % ways) for d in range(ways)])]
    unnamed x1, blocking collectives: 23.5 us -> 20.2 us
  transfers between devices with their start and end apart: 2 -> 8, of which waited for: 2 -> 6; matrix products, arithmetic and copies ran while one was open for 4% -> 5% of each run, Pallas kernels for 0% -> 0%
where the time goes in v1:
time: 248 us; the launch traced here: 247 us
  waiting for transfers between devices  153 us (62%)
  blocking collectives  25.9 us (10%)
  matrix products  21.6 us (9%)
  between operations  16.4 us (7%)
  starting transfers between devices  13 us (5%)
  local copies, waits for them, and re-layouts  10.3 us (4%)
  other arithmetic  7.03 us (3%)
    reduce_scatter x1, waiting for transfers between devices, per_device(): lax.psum_scatter(jnp.dot(normed, w_out, preferred_element_type=jnp.float3...  137 us
    unnamed x1, blocking collectives  20.2 us
    ppermute x3, waiting for transfers between devices, gather_around(): lax.ppermute(going_down, axis, [(d, (d - 1) % ways) for d in range(ways)])  12.3 us
    dot_general x1, matrix products, per_device(): jnp.dot(normed, w_out, preferred_element_type=jnp.float32)  11.9 us
    ppermute x4, starting transfers between devices, gather_around(): lax.ppermute(going_up, axis, [(d, (d + 1) % ways) for d in range(ways)])  9.86 us
    dot_general x1, matrix products, per_device(): jnp.einsum('hts,she->the', weights, values, preferred_element_type=jnp.fl...  6.95 us
    psum x1, blocking collectives, per_device(): squares = lax.psum(jnp.sum(attention * attention, axis=1), 'head')  5.67 us
  transfers between devices with their start and end apart: 8, of which 6 were waited for; matrix products, arithmetic and copies ran while one was open for 5% of the time, Pallas kernels for 0%

profile of v1, /device:TPU:0, one launch (start us, length us, event | category | flops | bytes accessed | tf_op | source)
XLA Modules:
  0.0 247.1 jit_solution(16930334126921008035)
XLA Ops:
  6.5 0.8 reshape.72
  7.4 1.1 reduce-window.6
  9.2 2.3 copy.31
  11.5 1.2 copy.32
  12.9 0.9 copy-done.1
  14.1 1.6 constant_dynamic-update-slice_fusion.7
  15.7 3.0 %collective-permute-start = (f32[1,4,128,128]{3,2,1,0:T(8,128)}, f32[1,4,128,128]{3,2,1,0:T(8,128)}, u32[]{:S(2)}, u32[]{:S(2)}) collective-permute-start(f32[1,4,128,128]{3,2,1,0:T(8,128)} %get-tuple-element.10), channel_id=1, source_target_pairs={{0,4},{4,8},{8,12},{12,16},{16,20},{20,24},{24,28},{28,0},{1,5},{5... | collective-permute-start | bytes 786440 | tf_op jit(solution)/shard_map/ppermute | solution.py:13
  18.6 3.0 %collective-permute-start.1 = (f32[1,4,128,128]{3,2,1,0:T(8,128)}, f32[1,4,128,128]{3,2,1,0:T(8,128)}, u32[]{:S(2)}, u32[]{:S(2)}) collective-permute-start(f32[1,4,128,128]{3,2,1,0:T(8,128)} %get-tuple-element.10), channel_id=1, source_target_pairs={{0,28},{4,0},{8,4},{12,8},{16,12},{20,16},{24,20},{28,24},{1,29},{... | collective-permute-start | bytes 786440 | tf_op jit(solution)/shard_map/ppermute | solution.py:16
  21.9 6.9 %fusion = f32[4,768,128]{1,2,0:T(8,128)} fusion(bf16[768,4,128]{0,2,1:T(8,128)(2,1)} %bitcast.52, f32[4,768]{1,0:T(4,128)S(1)} %get-tuple-element.8, pred[768,768]{1,0:T(8,128)(4,1)S(1)} %iota_compare_fusion, bf16[768,4,128]{0,2,1:T(8,128)(2,1)} %bitcast.50, bf16[768,512]{1,0:T(8,128)(2,1)S(1)} %copy-done), kind=kOutput, calls=%fused_computation.1 | convolution fusion | flops 1222115328 | bytes 4534272 | tf_op jit(solution)/shard_map/hts,she->the/dot_general | solution.py:44
  30.1 2.5 %collective-permute-start.2 = (f32[1,4,128,128]{3,2,1,0:T(8,128)}, f32[1,4,128,128]{3,2,1,0:T(8,128)S(1)}, u32[]{:S(2)}, u32[]{:S(2)}) collective-permute-start(f32[1,4,128,128]{3,2,1,0:T(8,128)} %collective-permute-done), channel_id=1, source_target_pairs={{0,4},{4,8},{8,12},{12,16},{16,20},{20,24},{24,28},{28,0},{1,5},{5... | collective-permute-start | bytes 786440 | tf_op jit(solution)/shard_map/ppermute | solution.py:13
  32.6 0.7 iota_compare_fusion.2
  36.8 20.2 %all-reduce = f32[32]{0:T(128)S(1)} all-reduce(f32[32]{0:T(128)S(1)} %dynamic-update-slice), channel_id=2, replica_groups=mesh['seg'=8,'head'=4] {'seg'}, use_global_device_ids=true, to_apply=%add | all-reduce | flops 32 | bytes 256
  58.1 1.9 collective-permute-start.4
  60.1 1.0 constant_dynamic-update-slice_fusion.6
  61.0 1.0 constant_dynamic-update-slice_fusion.5
  62.0 8.7 %collective-permute-done.3 = f32[1,4,128,128]{3,2,1,0:T(8,128)S(1)} collective-permute-done((f32[1,4,128,128]{3,2,1,0:T(8,128)}, f32[1,4,128,128]{3,2,1,0:T(8,128)S(1)}, u32[]{:S(2)}, u32[]{:S(2)}) %collective-permute-start.3) | collective-permute-done | bytes 262176 | tf_op jit(solution)/shard_map/ppermute | solution.py:16
  70.9 2.5 %collective-permute-start.6 = (f32[1,4,128,128]{3,2,1,0:T(8,128)S(1)}, f32[1,4,128,128]{3,2,1,0:T(8,128)S(1)}, u32[]{:S(2)}, u32[]{:S(2)}) collective-permute-start(f32[1,4,128,128]{3,2,1,0:T(8,128)S(1)} %collective-permute-done.4), channel_id=1, source_target_pairs={{0,4},{4,8},{8,12},{12,16},{16,20},{20,24},{24,28},{28,0},{1,5},{5... | collective-permute-start | bytes 786440 | tf_op jit(solution)/shard_map/ppermute | solution.py:13
  73.4 3.6 %collective-permute-done.5 = f32[1,4,128,128]{3,2,1,0:T(8,128)S(1)} collective-permute-done((f32[1,4,128,128]{3,2,1,0:T(8,128)S(1)}, f32[1,4,128,128]{3,2,1,0:T(8,128)S(1)}, u32[]{:S(2)}, u32[]{:S(2)}) %collective-permute-start.5) | collective-permute-done | bytes 262176 | tf_op jit(solution)/shard_map/ppermute | solution.py:16
  77.1 2.8 %collective-permute-done.6 = f32[1,4,128,128]{3,2,1,0:T(8,128)S(1)} collective-permute-done((f32[1,4,128,128]{3,2,1,0:T(8,128)S(1)}, f32[1,4,128,128]{3,2,1,0:T(8,128)S(1)}, u32[]{:S(2)}, u32[]{:S(2)}) %collective-permute-start.6) | collective-permute-done | bytes 262176 | tf_op jit(solution)/shard_map/ppermute | solution.py:13
  80.4 1.1 multiply_reduce_fusion
  81.5 5.7 %psum.7 = f32[768]{0:T(1024)S(1)} all-reduce(f32[768]{0:T(1024)S(1)} %get-tuple-element.11), channel_id=1, replica_groups=mesh['seg'=8,'head'=4] {'head'}, use_global_device_ids=true, to_apply=%region_6.7 | all-reduce | flops 768 | bytes 6144 | tf_op jit(solution)/shard_map/psum | solution.py:65
  87.4 11.9 %fusion.24 = f32[768,6144]{1,0:T(8,128)} fusion(bf16[768,512]{0,1:T(8,128)(2,1)S(1)} %fusion.5, bf16[512,6144]{1,0:T(8,128)(2,1)} %param.13), kind=kOutput, calls=%fused_computation.45 | convolution fusion | flops 4831838208 | bytes 25952256 | tf_op jit(solution)/shard_map/dot_general | solution.py:70
  99.3 136.9 %reduce-scatter.2.cloned.1.call-done = f32[192,6144]{1,0:T(8,128)} async-done(((f32[768,6144]{1,0:T(8,128)}), f32[192,6144]{1,0:T(8,128)}) %reduce-scatter.2.cloned.1.call-update) | async-done | bytes 4718608 | tf_op jit(solution)/shard_map/reduce_scatter | solution.py:69
  236.2 4.1 %convert_element_type.17 = bf16[192,6144]{1,0:T(8,128)(2,1)} convert(f32[192,6144]{1,0:T(8,128)} %reduce-scatter.2.cloned.1.call-done) | non-fusion elementwise | flops 1179648 | bytes 7077888 | tf_op jit(solution)/shard_map/convert_element_type | solution.py:75
  (48 shorter events, 5.2 us)
Async XLA Ops:
  6.5 15.3 %copy-start = (bf16[768,512]{1,0:T(8,128)(2,1)S(1)}, bf16[768,512]{1,0:T(8,128)(2,1)}, u32[]{:S(2)}) copy-start(bf16[768,512]{1,0:T(8,128)(2,1)} %param.7) | copy-start | bytes 2359300
  6.5 5.0 %copy-start.4 = (bf16[768,512]{1,0:T(8,128)(2,1)S(1)}, bf16[768,512]{1,0:T(8,128)(2,1)}, u32[]{:S(2)}) copy-start(bf16[768,512]{1,0:T(8,128)(2,1)} %param.9) | copy-start | bytes 2359300
  6.5 229.6 %reduce-scatter.2.cloned.1.call-start = ((), (), s32[]{:S(2)}) async-start(), calls=%async_computation.1 | async-start | bytes 23592960 | tf_op jit(solution)/shard_map/reduce_scatter | solution.py:69
  12.7 1.1 copy-start.1
  12.7 1.4 copy-start.2
  15.7 14.5 %collective-permute-start = (f32[1,4,128,128]{3,2,1,0:T(8,128)}, f32[1,4,128,128]{3,2,1,0:T(8,128)}, u32[]{:S(2)}, u32[]{:S(2)}) collective-permute-start(f32[1,4,128,128]{3,2,1,0:T(8,128)} %get-tuple-element.10), channel_id=1, source_target_pairs={{0,4},{4,8},{8,12},{12,16},{16,20},{20,24},{24,28},{28,0},{1,5},{5... | collective-permute-start | bytes 786440 | tf_op jit(solution)/shard_map/ppermute | solution.py:13
  18.6 39.2 %collective-permute-start.1 = (f32[1,4,128,128]{3,2,1,0:T(8,128)}, f32[1,4,128,128]{3,2,1,0:T(8,128)}, u32[]{:S(2)}, u32[]{:S(2)}) collective-permute-start(f32[1,4,128,128]{3,2,1,0:T(8,128)} %get-tuple-element.10), channel_id=1, source_target_pairs={{0,28},{4,0},{8,4},{12,8},{16,12},{20,16},{24,20},{28,24},{1,29},{... | collective-permute-start | bytes 786440 | tf_op jit(solution)/shard_map/ppermute | solution.py:16
  21.9 7.0 %copy-start.6 = (s32[8]{0:T(128)S(1)}, s32[8]{0:T(128)}, u32[]{:S(2)}) copy-start(s32[8]{0:T(128)} %param.11) | copy-start | bytes 100
  21.9 13.5 %copy-start.7 = (u32[32]{0:T(128)S(1)}, u32[32]{0:T(128)}, u32[]{:S(2)}) copy-start(u32[32]{0:T(128)} %constant.78) | copy-start | bytes 388
  30.1 28.0 %collective-permute-start.2 = (f32[1,4,128,128]{3,2,1,0:T(8,128)}, f32[1,4,128,128]{3,2,1,0:T(8,128)S(1)}, u32[]{:S(2)}, u32[]{:S(2)}) collective-permute-start(f32[1,4,128,128]{3,2,1,0:T(8,128)} %collective-permute-done), channel_id=1, source_target_pairs={{0,4},{4,8},{8,12},{12,16},{16,20},{20,24},{24,28},{28,0},{1,5},{5... | collective-permute-start | bytes 786440 | tf_op jit(solution)/shard_map/ppermute | solution.py:13
  57.9 12.8 %collective-permute-start.3 = (f32[1,4,128,128]{3,2,1,0:T(8,128)}, f32[1,4,128,128]{3,2,1,0:T(8,128)S(1)}, u32[]{:S(2)}, u32[]{:S(2)}) collective-permute-start(f32[1,4,128,128]{3,2,1,0:T(8,128)} %collective-permute-done.1), channel_id=1, source_target_pairs={{0,28},{4,0},{8,4},{12,8},{16,12},{20,16},{24,20},{28,24},{1,29},{... | collective-permute-start | bytes 786440 | tf_op jit(solution)/shard_map/ppermute | solution.py:16
  58.1 12.7 %collective-permute-start.4 = (f32[1,4,128,128]{3,2,1,0:T(8,128)S(1)}, f32[1,4,128,128]{3,2,1,0:T(8,128)S(1)}, u32[]{:S(2)}, u32[]{:S(2)}) collective-permute-start(f32[1,4,128,128]{3,2,1,0:T(8,128)S(1)} %collective-permute-done.2), channel_id=1, source_target_pairs={{0,4},{4,8},{8,12},{12,16},{16,20},{20,24},{24,28},{28,0},{1,5},{5... | collective-permute-start | bytes 786440 | tf_op jit(solution)/shard_map/ppermute | solution.py:13
  70.7 6.4 %collective-permute-start.5 = (f32[1,4,128,128]{3,2,1,0:T(8,128)S(1)}, f32[1,4,128,128]{3,2,1,0:T(8,128)S(1)}, u32[]{:S(2)}, u32[]{:S(2)}) collective-permute-start(f32[1,4,128,128]{3,2,1,0:T(8,128)S(1)} %collective-permute-done.3), channel_id=1, source_target_pairs={{0,28},{4,0},{8,4},{12,8},{16,12},{20,16},{24,20},{28,24},{1,29},{... | collective-permute-start | bytes 786440 | tf_op jit(solution)/shard_map/ppermute | solution.py:16
  70.9 9.1 %collective-permute-start.6 = (f32[1,4,128,128]{3,2,1,0:T(8,128)S(1)}, f32[1,4,128,128]{3,2,1,0:T(8,128)S(1)}, u32[]{:S(2)}, u32[]{:S(2)}) collective-permute-start(f32[1,4,128,128]{3,2,1,0:T(8,128)S(1)} %collective-permute-done.4), channel_id=1, source_target_pairs={{0,4},{4,8},{8,12},{12,16},{16,20},{20,24},{24,28},{28,0},{1,5},{5... | collective-permute-start | bytes 786440 | tf_op jit(solution)/shard_map/ppermute | solution.py:13
  73.4 7.0 %copy-start.3 = (f32[4,768,128]{1,2,0:T(8,128)S(1)}, f32[4,768,128]{1,2,0:T(8,128)}, u32[]{:S(2)}) copy-start(f32[4,768,128]{1,2,0:T(8,128)} %fusion) | copy-start | bytes 4718596
  80.4 6.8 %copy-start.5 = (f32[512]{0:T(512)S(1)}, f32[512]{0:T(512)}, u32[]{:S(2)}) copy-start(f32[512]{0:T(512)} %param.12) | copy-start | bytes 6148
Sparse Core Ops, SparseCore 0:
  99.4 136.6 reduce-scatter.1
